TPU v7x, 128 devices: a whole 4x4x4 slice. The times are simulated.
128 devices in a mesh: group: 16 (over y_hi, x, core), mp: 8 (over z, y_lo).
Axes of the slice: x: 4, y: 4 (y_hi: 2, y_lo: 2; y = y_hi * 2 + y_lo), z: 4, core: 2. Of those that a mesh axis runs over, the one named last changes fastest.
Arguments:
- hidden_in: bfloat16 [8192, 1024], P('group'), may hold values from -8 to 8
- request_ids: int32 [8192], P('group'), may hold values from 63 to 8191, as said below
- w_qkv: float32 [1024, 3072], P(('group', 'mp')), may hold values from -1 to 1
- w_out: float32 [1024, 1024], P(('group', 'mp')), may hold values from -0.1875 to 0.1875
- w_up: float32 [1024, 4096], P(('group', 'mp')), may hold values from -0.1875 to 0.1875
- w_down: float32 [1024, 4096], P(('group', 'mp')), may hold values from -0.09375 to 0.09375
- ln1_gain: float32 [1024], replicated, may hold values from 0.25 to 1.75
- ln1_shift: float32 [1024], replicated, may hold values from -3 to 3
- ln2_gain: float32 [1024], replicated, may hold values from 0.25 to 1.75
- ln2_shift: float32 [1024], replicated, may hold values from -3 to 3
Outputs:
- hidden_out: bfloat16 [8192, 1024], P(('group', 'mp'))
- keys_cache: bfloat16 [8192, 1024], P('group', 'mp')
- values_cache: bfloat16 [8192, 1024], P('group', 'mp')
Inputs may be any that keep to these rules, and one draw needn't show every extreme that they name: `request_ids`: each slot holds the index of the last slot of its request. In groups 2i and 2i+1 (of 512 slots each) one request of exactly 512 slots ends the first group and begins the second, at least 64 of its slots in each; every other request lies within one aligned block of 64 slots, one or two requests a block, and some blocks hold one request of exactly 64 slots.
All inputs are finite; a program needn't handle non-finite values.
Results may differ from a plain program's by a relative error of at most 0.011.
Values may be sent and summed in bfloat16 or wider, within the bound.
No kernel may reach another device: no remote copies, remote signals or barrier semaphores. Data moves between devices by JAX's collectives and lax.ppermute only.
A program may use at most 64 MiB of HBM per device.

v0:
```python
import jax
import jax.numpy as jnp
from jax import lax
from jax.sharding import PartitionSpec as P

HD = 64
SHORT = 64


def swapped(value, axis, distance):
    return lax.ppermute(value, axis, [(i, i ^ 1 << distance) for i in range(lax.axis_size(axis))])


def layer_norm(values_in, norm_gain, norm_shift):
    center = values_in - jnp.mean(values_in, axis=-1, keepdims=True)
    spread = jnp.mean(center * center, axis=-1, keepdims=True)
    return center * lax.rsqrt(spread + 1e-05) * norm_gain + norm_shift


def body(
    hidden_in, request_ids, w_qkv, w_out, w_up, w_down, ln1_gain, ln1_shift, ln2_gain, ln2_shift
):
    groups = lax.axis_size("group")
    shards = lax.axis_size("mp")
    model_width = hidden_in.shape[1]
    local_width = model_width // shards
    local_hidden = w_up.shape[1] // shards
    tok_rows = hidden_in.shape[0]
    part_rows = w_qkv.shape[0]
    pieces = (
        w_qkv.astype(jnp.bfloat16).reshape(part_rows, 3, shards, local_width),
        w_out.astype(jnp.bfloat16).reshape(part_rows, 1, shards, local_width),
        w_up.astype(jnp.bfloat16).reshape(part_rows, 1, shards, local_hidden),
        w_down.astype(jnp.bfloat16).reshape(part_rows, 1, shards, local_hidden),
    )
    gathered = (
        lax.all_gather(pieces[0], "group", axis=0, tiled=True),
        lax.all_gather(pieces[1], "group", axis=0, tiled=True),
        lax.all_gather(pieces[2], "group", axis=0, tiled=True),
        lax.all_gather(pieces[3], "group", axis=0, tiled=True),
    )
    exchanged = (
        lax.all_to_all(gathered[0], "mp", split_axis=2, concat_axis=0, tiled=True),
        lax.all_to_all(gathered[1], "mp", split_axis=2, concat_axis=0, tiled=True),
        lax.all_to_all(gathered[2], "mp", split_axis=2, concat_axis=0, tiled=True),
        lax.all_to_all(gathered[3], "mp", split_axis=2, concat_axis=0, tiled=True),
    )
    served = tuple(
        (
            jnp.transpose(
                weight_piece.reshape(shards, groups, part_rows, -1), (1, 0, 2, 3)
            ).reshape(model_width, -1)
            for weight_piece in exchanged
        )
    )
    qkv_local, out_local, up_local, down_local = served
    projected = jnp.dot(hidden_in, qkv_local, preferred_element_type=jnp.float32)
    queries = projected[:, :local_width].astype(jnp.bfloat16)
    key_rows = projected[:, local_width : 2 * local_width].astype(jnp.bfloat16)
    value_rows = projected[:, 2 * local_width :].astype(jnp.bfloat16)
    partner_keys, partner_values = swapped((key_rows, value_rows), "group", 0)
    group_index = lax.axis_index("group")
    parity = group_index % 2
    long_id = jnp.where(parity == 0, request_ids[-1], request_ids[0])
    own_long = request_ids == long_id
    local_heads = local_width // HD
    score_scale = HD ** (-0.5)
    block_total = tok_rows // SHORT
    short_q = queries.reshape(block_total, SHORT, local_heads, HD)
    short_k = key_rows.reshape(block_total, SHORT, local_heads, HD)
    short_v = value_rows.reshape(block_total, SHORT, local_heads, HD)
    short_ids = request_ids.reshape(block_total, SHORT)
    short_scores = (
        jnp.einsum("bqhd,bkhd->bhqk", short_q, short_k, preferred_element_type=jnp.float32)
        * score_scale
    )
    short_mask = short_ids[:, :, None] == short_ids[:, None, :]
    short_scores = jnp.where(short_mask[:, None], short_scores, -1e30)
    short_peak = jnp.max(short_scores, axis=-1, keepdims=True)
    short_weights = jnp.exp(short_scores - short_peak).astype(jnp.bfloat16)
    short_totals = jnp.sum(short_weights.astype(jnp.float32), axis=-1)
    short_mixed = jnp.einsum(
        "bhqk,bkhd->bqhd", short_weights, short_v, preferred_element_type=jnp.float32
    )
    short_out = (
        (short_mixed / jnp.transpose(short_totals, (0, 2, 1))[:, :, :, None])
        .astype(jnp.bfloat16)
        .reshape(tok_rows, local_width)
    )
    first_keys = jnp.where(parity == 0, key_rows, partner_keys)
    second_keys = jnp.where(parity == 0, partner_keys, key_rows)
    first_values = jnp.where(parity == 0, value_rows, partner_values)
    second_values = jnp.where(parity == 0, partner_values, value_rows)
    pair_base = (group_index - parity) * tok_rows
    span_start = long_id - tok_rows + 1 - pair_base
    long_keys = lax.dynamic_slice_in_dim(
        jnp.concatenate([first_keys, second_keys], 0), span_start, tok_rows, 0
    ).reshape(tok_rows, local_heads, HD)
    long_values = lax.dynamic_slice_in_dim(
        jnp.concatenate([first_values, second_values], 0), span_start, tok_rows, 0
    ).reshape(tok_rows, local_heads, HD)
    query_rows = min(512, tok_rows)
    query_blocks = tok_rows // query_rows

    def long_attend(block_queries):
        heads_view = block_queries.reshape(query_rows, local_heads, HD)
        scores = (
            jnp.einsum("qhd,khd->hqk", heads_view, long_keys, preferred_element_type=jnp.float32)
            * score_scale
        )
        row_peak = jnp.max(scores, axis=-1, keepdims=True)
        weights = jnp.exp(scores - row_peak).astype(jnp.bfloat16)
        totals = jnp.sum(weights.astype(jnp.float32), axis=-1)
        mixed_heads = jnp.einsum(
            "hqk,khd->qhd", weights, long_values, preferred_element_type=jnp.float32
        )
        return (
            (mixed_heads / jnp.transpose(totals)[:, :, None])
            .astype(jnp.bfloat16)
            .reshape(query_rows, local_width)
        )

    def skipped(block_queries):
        return jnp.zeros((query_rows, local_width), jnp.bfloat16)

    def long_block(query_block):
        block_queries, block_long = query_block
        return lax.cond(jnp.any(block_long), long_attend, skipped, block_queries)

    long_out = lax.map(
        long_block,
        (
            queries.reshape(query_blocks, query_rows, local_width),
            own_long.reshape(query_blocks, query_rows),
        ),
    ).reshape(tok_rows, local_width)
    attended = jnp.where(own_long[:, None], long_out, short_out)
    share_rows = tok_rows // shards
    row_start = lax.axis_index("mp") * share_rows

    def combine(term_fn, residual, norm_gain, norm_shift):
        summed = lax.psum(term_fn(0, tok_rows), "mp")
        whole_rows = layer_norm(
            residual.astype(jnp.float32) + summed, norm_gain, norm_shift
        ).astype(jnp.bfloat16)
        normed = lax.dynamic_slice_in_dim(whole_rows, row_start, share_rows, 0)
        return (normed, whole_rows)

    def attn_term(row_begin, row_count):
        return lax.dot_general(
            attended, out_local, (((1,), (1,)), ((), ())), preferred_element_type=jnp.float32
        )

    attn_share, attn_normed = combine(attn_term, hidden_in, ln1_gain, ln1_shift)
    activated = jax.nn.gelu(
        jnp.dot(attn_normed, up_local, preferred_element_type=jnp.float32), approximate=False
    ).astype(jnp.bfloat16)

    def feed_term(row_begin, row_count):
        return lax.dot_general(
            activated, down_local, (((1,), (1,)), ((), ())), preferred_element_type=jnp.float32
        )

    final_share, unused = combine(feed_term, attn_normed, ln2_gain, ln2_shift)
    return (final_share, key_rows, value_rows)


def solution(mesh):
    in_specs = (
        P("group", None),
        P("group"),
        P(("group", "mp"), None),
        P(("group", "mp"), None),
        P(("group", "mp"), None),
        P(("group", "mp"), None),
        P(),
        P(),
        P(),
        P(),
    )
    out_specs = (P(("group", "mp"), None), P("group", "mp"), P("group", "mp"))
    return jax.shard_map(body, mesh=mesh, in_specs=in_specs, out_specs=out_specs, check_vma=False)
```

profile of v0, /device:TPU:1, one launch (start us, length us, event | category | flops | bytes accessed | tf_op | source)
XLA Modules:
  0.0 345.1 jit_solution(3405241490203082044)
XLA Ops:
  8.0 1.5 convert_element_type.73
  9.6 0.8 convert_bitcast_fusion.1
  10.4 27.8 %all_gather.13 = bf16[128,1,8,128]{3,0,1,2:T(8,128)(2,1)} all-gather(bf16[8,1,8,128]{3,0,1,2:T(8,128)(2,1)S(1)} %convert_bitcast_fusion.1), channel_id=1, replica_groups=mesh['group'=16,'mp'=8] {'group'}, dimensions={0}, use_global_device_ids=true | all-gather | bytes 278528 | tf_op jit(solution)/shard_map/all_gather | solution.py:38
  38.1 5.1 %all-to-all-start.1 = ((bf16[128,1,8,128]{3,0,1,2:T(8,128)(2,1)}), bf16[128,1,8,128]{3,0,1,2:T(8,128)(2,1)S(1)}, u32[]{:S(2)}, u32[]{:S(2)}) async-start(bf16[128,1,8,128]{3,0,1,2:T(8,128)(2,1)} %all_gather.13), calls=%async_computation.1 | async-start | bytes 524288 | tf_op jit(solution)/shard_map/all_to_all | solution.py:44
  43.3 0.9 convert_bitcast_fusion
  44.2 22.1 %all_gather.12 = bf16[128,3,8,128]{3,2,1,0:T(8,128)(2,1)S(1)} all-gather(bf16[8,3,8,128]{3,2,1,0:T(8,128)(2,1)S(1)} %bitcast.100), channel_id=1, replica_groups=mesh['group'=16,'mp'=8] {'group'}, dimensions={0}, use_global_device_ids=true | all-gather | bytes 835584 | tf_op jit(solution)/shard_map/all_gather | solution.py:37
  66.3 1.1 copy.76
  67.4 5.8 %all-to-all-start = ((bf16[128,3,8,128]{3,0,1,2:T(8,128)(2,1)}), bf16[128,3,8,128]{3,0,1,2:T(8,128)(2,1)S(1)}, u32[]{:S(2)}, u32[]{:S(2)}) async-start(bf16[128,3,8,128]{3,0,1,2:T(8,128)(2,1)} %copy.76), calls=%async_computation | async-start | bytes 1572864 | tf_op jit(solution)/shard_map/all_to_all | solution.py:43
  73.2 0.6 convert_element_type.75
  74.1 0.6 fusion.98
  75.9 0.6 fusion.96
  77.4 8.3 %all-to-all-done = bf16[128,3,8,128]{3,0,1,2:T(8,128)(2,1)S(1)} async-done(((bf16[128,3,8,128]{3,0,1,2:T(8,128)(2,1)}), bf16[128,3,8,128]{3,0,1,2:T(8,128)(2,1)S(1)}, u32[]{:S(2)}, u32[]{:S(2)}) %all-to-all-start) | async-done | bytes 786464 | tf_op jit(solution)/shard_map/all_to_all | solution.py:43
  85.8 0.7 copy.77
  86.5 0.7 reshape.140
  87.3 0.4 copy-done.1
  87.7 0.7 convolution_convert_fusion
  88.5 1.4 collective-permute-start
  90.4 0.3 fusion.9
  90.7 0.1 convert_reduce_fusion.1
  90.8 0.6 copy-done.12
  91.4 1.5 fusion.10
  92.9 0.2 copy.86
  93.1 0.2 reshape.145
  93.5 2.0 conditional.1
  93.8 0.2 constant_dynamic-slice_fusion
  94.1 0.5 bitcast_reduce_fusion
  94.6 0.4 convert_reduce_fusion
  95.0 0.5 fusion.3
  95.5 1.8 fusion.61
  97.3 3.6 %all-to-all-start.2 = ((bf16[128,1,8,512]{3,0,1,2:T(8,128)(2,1)}), bf16[128,1,8,512]{3,0,1,2:T(8,128)(2,1)S(1)}, u32[]{:S(2)}, u32[]{:S(2)}) async-start(bf16[128,1,8,512]{3,0,1,2:T(8,128)(2,1)} %all-gather.3.cloned.1.call-done), calls=%async_computation.2 | async-start | bytes 2097152 | tf_op jit(solution)/shard_map/all_to_all | solution.py:45
  100.9 30.2 %all-gather.5.cloned.1.call-done = bf16[128,1,8,512]{3,0,1,2:T(8,128)(2,1)} async-done(((bf16[8,1,8,512]{3,0,1,2:T(8,128)(2,1)}), bf16[128,1,8,512]{3,0,1,2:T(8,128)(2,1)}) %all-gather.5.cloned.1.call-update) | async-done | bytes 1048592 | tf_op jit(solution)/shard_map/all_gather | solution.py:40
  131.1 4.2 %all-to-all-start.3 = ((bf16[128,1,8,512]{3,0,1,2:T(8,128)(2,1)}), bf16[128,1,8,512]{3,0,1,2:T(8,128)(2,1)S(1)}, u32[]{:S(2)}, u32[]{:S(2)}) async-start(bf16[128,1,8,512]{3,0,1,2:T(8,128)(2,1)} %all-gather.5.cloned.1.call-done), calls=%async_computation.3 | async-start | bytes 2097152 | tf_op jit(solution)/shard_map/all_to_all | solution.py:46
  135.2 0.2 all-reduce.5.cloned.1.call-start
  135.5 1.1 copy.88
  136.6 26.0 %all-to-all-done.3 = bf16[128,1,8,512]{3,0,1,2:T(8,128)(2,1)S(1)} async-done(((bf16[128,1,8,512]{3,0,1,2:T(8,128)(2,1)}), bf16[128,1,8,512]{3,0,1,2:T(8,128)(2,1)S(1)}, u32[]{:S(2)}, u32[]{:S(2)}) %all-to-all-start.3) | async-done | bytes 1048608 | tf_op jit(solution)/shard_map/all_to_all | solution.py:46
  162.6 1.1 copy.89
  163.7 56.5 %all-reduce.3.cloned.1.call-done = f32[512,1024]{1,0:T(8,128)} async-done(((f32[512,1024]{1,0:T(8,128)}), f32[512,1024]{1,0:T(8,128)}) %all-reduce.3.cloned.1.call-update) | async-done | bytes 2097168 | tf_op jit(solution)/shard_map/psum | solution.py:142
  220.2 2.0 fusion.21
  222.3 0.2 copy-done
  222.4 0.5 multiply_reduce_fusion.1
  223.0 0.5 add_convert_fusion
  223.5 0.7 copy-done.5
  224.2 5.9 %fusion.22 = f32[512,1024]{1,0:T(8,128)} fusion(bf16[1024,512]{1,0:T(8,128)(2,1)} %bitcast.91, bf16[512,1024]{1,0:T(8,128)(2,1)S(1)} %add_convert_fusion, bf16[1024,512]{1,0:T(8,128)(2,1)S(1)} %bitcast.90), kind=kOutput, calls=%fused_computation.44 | convolution fusion | flops 1090781184 | bytes 5242880 | tf_op jit(solution)/shard_map/dot_general | solution.py:160
  230.2 103.9 %all-reduce.5.cloned.1.call-done = f32[512,1024]{1,0:T(8,128)} async-done(((f32[512,1024]{1,0:T(8,128)}), f32[512,1024]{1,0:T(8,128)}) %all-reduce.5.cloned.1.call-update) | async-done | bytes 2097168 | tf_op jit(solution)/shard_map/psum | solution.py:142
  334.0 2.0 fusion.7
  336.1 0.2 copy-done.2
  336.3 0.5 multiply_reduce_fusion
  337.0 0.8 fusion.56
  (54 shorter events, 2.1 us)
Async XLA Ops:
  8.0 89.3 %all-gather.3.cloned.1.call-start = ((), (), s32[]{:S(2)}) async-start(), calls=%async_computation.5 | async-start | bytes 1114112 | tf_op jit(solution)/shard_map/all_gather | solution.py:39
  38.1 29.3 %all-to-all-start.1 = ((bf16[128,1,8,128]{3,0,1,2:T(8,128)(2,1)}), bf16[128,1,8,128]{3,0,1,2:T(8,128)(2,1)S(1)}, u32[]{:S(2)}, u32[]{:S(2)}) async-start(bf16[128,1,8,128]{3,0,1,2:T(8,128)(2,1)} %all_gather.13), calls=%async_computation.1 | async-start | bytes 524288 | tf_op jit(solution)/shard_map/all_to_all | solution.py:44
  43.3 29.9 %copy-start.6 = (f32[8,4096]{1,0:T(8,128)S(1)}, f32[8,4096]{1,0:T(8,128)}, u32[]{:S(2)}) copy-start(f32[8,4096]{1,0:T(8,128)} %param.17) | copy-start | bytes 393220
  44.2 29.8 %copy-start.7 = (s32[512]{0:T(512)S(1)}, s32[512]{0:T(512)}, u32[]{:S(2)}) copy-start(s32[512]{0:T(512)} %param.13) | copy-start | bytes 6148
  67.4 18.4 %all-to-all-start = ((bf16[128,3,8,128]{3,0,1,2:T(8,128)(2,1)}), bf16[128,3,8,128]{3,0,1,2:T(8,128)(2,1)S(1)}, u32[]{:S(2)}, u32[]{:S(2)}) async-start(bf16[128,3,8,128]{3,0,1,2:T(8,128)(2,1)} %copy.76), calls=%async_computation | async-start | bytes 1572864 | tf_op jit(solution)/shard_map/all_to_all | solution.py:43
  73.2 57.9 %all-gather.5.cloned.1.call-start = ((), (), s32[]{:S(2)}) async-start(), calls=%async_computation.6 | async-start | bytes 1114112 | tf_op jit(solution)/shard_map/all_gather | solution.py:40
  73.9 146.3 %all-reduce.3.cloned.1.call-start = ((), (), s32[]{:S(2)}) async-start(), calls=%async_computation.4 | async-start | bytes 4194304 | tf_op jit(solution)/shard_map/psum | solution.py:142
  86.4 1.2 copy-start.1
  88.5 4.9 %copy-start.3 = (bf16[512,128]{1,0:T(8,128)(2,1)}, bf16[512,128]{1,0:T(8,128)(2,1)S(1)}, u32[]{:S(2)}) copy-start(bf16[512,128]{1,0:T(8,128)(2,1)S(1)} %get-tuple-element.157) | copy-start | bytes 393220
  88.5 4.9 %copy-start.4 = (bf16[512,128]{1,0:T(8,128)(2,1)}, bf16[512,128]{1,0:T(8,128)(2,1)S(1)}, u32[]{:S(2)}) copy-start(bf16[512,128]{1,0:T(8,128)(2,1)S(1)} %get-tuple-element.159) | copy-start | bytes 393220
  88.5 4.9 %collective-permute-start = (bf16[512,128]{1,0:T(8,128)(2,1)S(1)}, bf16[512,128]{1,0:T(8,128)(2,1)S(1)}, u32[]{:S(2)}, u32[]{:S(2)}) collective-permute-start(bf16[512,128]{1,0:T(8,128)(2,1)S(1)} %get-tuple-element.159), channel_id=1, source_target_pairs={{0,8},{8,0},{16,24},{24,16},{32,40},{40,32},{48,56},{56,48},{64,72... | collective-permute-start | bytes 393224 | tf_op jit(solution)/shard_map/ppermute | solution.py:11
  90.0 3.3 collective-permute-start.1
  90.6 0.8 copy-start.12
  97.3 33.8 %all-to-all-start.2 = ((bf16[128,1,8,512]{3,0,1,2:T(8,128)(2,1)}), bf16[128,1,8,512]{3,0,1,2:T(8,128)(2,1)S(1)}, u32[]{:S(2)}, u32[]{:S(2)}) async-start(bf16[128,1,8,512]{3,0,1,2:T(8,128)(2,1)} %all-gather.3.cloned.1.call-done), calls=%async_computation.2 | async-start | bytes 2097152 | tf_op jit(solution)/shard_map/all_to_all | solution.py:45
  131.1 31.5 %all-to-all-start.3 = ((bf16[128,1,8,512]{3,0,1,2:T(8,128)(2,1)}), bf16[128,1,8,512]{3,0,1,2:T(8,128)(2,1)S(1)}, u32[]{:S(2)}, u32[]{:S(2)}) async-start(bf16[128,1,8,512]{3,0,1,2:T(8,128)(2,1)} %all-gather.5.cloned.1.call-done), calls=%async_computation.3 | async-start | bytes 2097152 | tf_op jit(solution)/shard_map/all_to_all | solution.py:46
  135.2 198.8 %all-reduce.5.cloned.1.call-start = ((), (), s32[]{:S(2)}) async-start(), calls=%async_computation.7 | async-start | bytes 4194304 | tf_op jit(solution)/shard_map/psum | solution.py:142
  220.2 2.2 copy-start
  222.2 0.7 copy-start.8
  222.3 0.7 copy-start.9
  223.0 1.2 copy-start.5
  334.0 2.2 copy-start.2
  336.3 0.7 copy-start.10
  336.3 0.7 copy-start.11
Sparse Core Ops, SparseCore 0:
  11.1 50.7 all-gather.2
  76.8 54.1 all-gather.4
Sparse Core Ops, SparseCore 1:
  97.4 122.8 all-reduce.2
  230.3 103.7 all-reduce.4
where the time goes:
time: 346 us; the launch traced here: 345 us
  waiting for transfers between devices  225 us (65%)
  blocking collectives  49.9 us (14%)
  starting transfers between devices  20.4 us (6%)
  between operations  17.7 us (5%)
  other arithmetic  11.5 us (3%)
  matrix products  11.2 us (3%)
  local copies, waits for them, and re-layouts  9.31 us (3%)
    psum x2, waiting for transfers between devices, combine(): summed = lax.psum(term_fn(0, tok_rows), 'mp')  160 us
    all_gather x1, waiting for transfers between devices, body(): lax.all_gather(pieces[3], 'group', axis=0, tiled=True)  30.2 us
    all_gather x1, blocking collectives, body(): lax.all_gather(pieces[1], 'group', axis=0, tiled=True)  27.8 us
    all_to_all x1, waiting for transfers between devices, body(): lax.all_to_all(gathered[3], 'mp', split_axis=2, concat_axis=0, tiled=True)  26 us
    all_gather x1, blocking collectives, body(): lax.all_gather(pieces[0], 'group', axis=0, tiled=True)  22.1 us
    all_to_all x1, waiting for transfers between devices, body(): lax.all_to_all(gathered[0], 'mp', split_axis=2, concat_axis=0, tiled=True)  8.33 us
  transfers between devices with their start and end apart: 10, of which 5 were waited for; matrix products, arithmetic and copies ran while one was open for 5% of the time, Pallas kernels for 0%

commit v1 on v0

--- a/solution.py
+++ b/solution.py
@@ -5,6 +5,9 @@
 
 HD = 64
 SHORT = 64
+launch_object_over_axis = lambda panel, group_axis: jax.lax.all_gather(
+    panel, axis_name=group_axis
+).sum(axis=0)
 
 
 def swapped(value, axis, distance):
@@ -139,7 +142,7 @@
     row_start = lax.axis_index("mp") * share_rows
 
     def combine(term_fn, residual, norm_gain, norm_shift):
-        summed = lax.psum(term_fn(0, tok_rows), "mp")
+        summed = launch_object_over_axis(term_fn(0, tok_rows), "mp")
         whole_rows = layer_norm(
             residual.astype(jnp.float32) + summed, norm_gain, norm_shift
         ).astype(jnp.bfloat16)

time: 346 us -> 816 us (2.36)
  waiting for transfers between devices: 225 us -> 684 us
  other arithmetic: 11.5 us -> 24.9 us
    all_gather x0 -> x2, waiting for transfers between devices: none -> 633 us  [jax.lax.all_gather(panel, axis_name=group_axis).sum(axis=0)]
    psum x2 -> x0, waiting for transfers between devices: 160 us -> none  [combine(): summed = lax.psum(term_fn(0, tok_rows), 'mp')]
    reduce_sum x0 -> x2, other arithmetic: none -> 16 us  [launch_object_over_axis = lambda panel, group_axis: jax.lax.all_gather(pa...]
  transfers between devices with their start and end apart: 10 -> 10, of which waited for: 5 -> 5; matrix products, arithmetic and copies ran while one was open for 5% -> 2% of each run, Pallas kernels for 0% -> 0%
where the time goes in v1:
time: 816 us
  waiting for transfers between devices  684 us (84%)
  blocking collectives  49.9 us (6%)
  other arithmetic  24.9 us (3%)
  starting transfers between devices  20.9 us (3%)
  between operations  16 us (2%)
  matrix products  11.8 us (1%)
  local copies, waits for them, and re-layouts  8.4 us (1%)
    all_gather x2, waiting for transfers between devices, jax.lax.all_gather(panel, axis_name=group_axis).sum(axis=0)  633 us
    all_gather x1, blocking collectives, body(): lax.all_gather(pieces[1], 'group', axis=0, tiled=True)  27.7 us
    all_gather x1, waiting for transfers between devices, body(): lax.all_gather(pieces[3], 'group', axis=0, tiled=True)  22.5 us
    all_gather x1, blocking collectives, body(): lax.all_gather(pieces[0], 'group', axis=0, tiled=True)  22.1 us
    all_to_all x1, waiting for transfers between devices, body(): lax.all_to_all(gathered[3], 'mp', split_axis=2, concat_axis=0, tiled=True)  19.4 us
  transfers between devices with their start and end apart: 10, of which 5 were waited for; matrix products, arithmetic and copies ran while one was open for 2% of the time, Pallas kernels for 0%

profile of v1, /device:TPU:1, one launch (start us, length us, event | category | flops | bytes accessed | tf_op | source)
XLA Modules:
  0.0 815.8 jit_solution(12789432771344062430)
XLA Ops:
  7.2 1.5 convert_element_type.73
  8.8 0.8 convert_bitcast_fusion.1
  9.5 27.7 %all_gather.25 = bf16[128,1,8,128]{3,0,1,2:T(8,128)(2,1)} all-gather(bf16[8,1,8,128]{3,0,1,2:T(8,128)(2,1)S(1)} %convert_bitcast_fusion.1), channel_id=1, replica_groups=mesh['group'=16,'mp'=8] {'group'}, dimensions={0}, use_global_device_ids=true | all-gather | bytes 278528 | tf_op jit(solution)/shard_map/all_gather | solution.py:41
  37.3 5.1 all-to-all-start.1
  42.4 0.9 convert_bitcast_fusion
  43.4 22.1 %all_gather.24 = bf16[128,3,8,128]{3,2,1,0:T(8,128)(2,1)S(1)} all-gather(bf16[8,3,8,128]{3,2,1,0:T(8,128)(2,1)S(1)} %bitcast.104), channel_id=1, replica_groups=mesh['group'=16,'mp'=8] {'group'}, dimensions={0}, use_global_device_ids=true | all-gather | bytes 835584 | tf_op jit(solution)/shard_map/all_gather | solution.py:40
  65.5 1.1 copy.76
  66.6 5.7 all-to-all-start
  72.4 0.6 convert_element_type.75
  73.2 0.6 fusion.98
  75.1 0.6 fusion.96
  76.6 8.3 %all-to-all-done = bf16[128,3,8,128]{3,0,1,2:T(8,128)(2,1)S(1)} async-done(((bf16[128,3,8,128]{3,0,1,2:T(8,128)(2,1)}), bf16[128,3,8,128]{3,0,1,2:T(8,128)(2,1)S(1)}, u32[]{:S(2)}, u32[]{:S(2)}) %all-to-all-start) | async-done | bytes 786464 | tf_op jit(solution)/shard_map/all_to_all | solution.py:46
  84.9 0.7 copy.77
  85.6 0.7 reshape.140
  86.4 0.4 copy-done
  86.8 0.7 convolution_convert_fusion
  87.6 1.4 collective-permute-start
  89.5 0.3 fusion.9
  89.8 0.1 convert_reduce_fusion.1
  90.0 0.6 copy-done.10
  90.6 1.5 fusion.10
  92.1 0.2 copy.86
  92.3 0.2 reshape.145
  92.7 2.0 conditional.1
  93.0 0.2 constant_dynamic-slice_fusion
  93.3 0.5 bitcast_reduce_fusion
  93.8 0.4 convert_reduce_fusion
  94.2 0.5 fusion.3
  94.6 1.8 fusion.61
  96.5 3.6 all-to-all-start.2
  100.1 22.5 %all-gather.9.cloned.1.call-done = bf16[128,1,8,512]{3,0,1,2:T(8,128)(2,1)} async-done(((bf16[8,1,8,512]{3,0,1,2:T(8,128)(2,1)}), bf16[128,1,8,512]{3,0,1,2:T(8,128)(2,1)}) %all-gather.9.cloned.1.call-update) | async-done | bytes 1048592 | tf_op jit(solution)/shard_map/all_gather | solution.py:43
  122.6 4.7 all-to-all-start.3
  127.2 0.2 all-gather.13.cloned.1.call-start
  127.5 1.1 copy.88
  128.6 19.4 %all-to-all-done.3 = bf16[128,1,8,512]{3,0,1,2:T(8,128)(2,1)S(1)} async-done(((bf16[128,1,8,512]{3,0,1,2:T(8,128)(2,1)}), bf16[128,1,8,512]{3,0,1,2:T(8,128)(2,1)S(1)}, u32[]{:S(2)}, u32[]{:S(2)}) %all-to-all-start.3) | async-done | bytes 1048608 | tf_op jit(solution)/shard_map/all_to_all | solution.py:49
  147.9 1.1 copy.89
  149.0 307.5 %all-gather.11.cloned.1.call-done = f32[4096,1024]{1,0:T(8,128)} async-done(((f32[512,1024]{1,0:T(8,128)}), f32[4096,1024]{1,0:T(8,128)}) %all-gather.11.cloned.1.call-update) | async-done | bytes 16777232 | tf_op jit(solution)/shard_map/all_gather | solution.py:8
  456.5 8.0 reduce_sum.77
  464.4 0.3 fusion.21
  464.8 0.4 multiply_reduce_fusion.1
  465.2 0.2 copy-done.6
  465.4 1.5 add_convert_fusion
  466.9 6.6 fusion.22
  473.5 325.9 %all-gather.13.cloned.1.call-done = f32[4096,1024]{1,0:T(8,128)} async-done(((f32[512,1024]{1,0:T(8,128)}), f32[4096,1024]{1,0:T(8,128)}) %all-gather.13.cloned.1.call-update) | async-done | bytes 16777232 | tf_op jit(solution)/shard_map/all_gather | solution.py:8
  799.4 8.0 reduce_sum.80
  807.5 0.3 fusion.7
  807.8 0.5 multiply_reduce_fusion
  808.5 0.8 fusion.56
  (52 shorter events, 2.0 us)
Async XLA Ops:
  7.2 89.3 %all-gather.7.cloned.1.call-start = ((), (), s32[]{:S(2)}) async-start(), calls=%async_computation.4 | async-start | bytes 1114112 | tf_op jit(solution)/shard_map/all_gather | solution.py:42
  37.3 29.3 %all-to-all-start.1 = ((bf16[128,1,8,128]{3,0,1,2:T(8,128)(2,1)}), bf16[128,1,8,128]{3,0,1,2:T(8,128)(2,1)S(1)}, u32[]{:S(2)}, u32[]{:S(2)}) async-start(bf16[128,1,8,128]{3,0,1,2:T(8,128)(2,1)} %all_gather.25), calls=%async_computation.1 | async-start | bytes 524288 | tf_op jit(solution)/shard_map/all_to_all | solution.py:47
  42.4 30.0 %copy-start.4 = (f32[8,4096]{1,0:T(8,128)S(1)}, f32[8,4096]{1,0:T(8,128)}, u32[]{:S(2)}) copy-start(f32[8,4096]{1,0:T(8,128)} %param.17) | copy-start | bytes 393220
  43.4 29.8 %copy-start.5 = (s32[512]{0:T(512)S(1)}, s32[512]{0:T(512)}, u32[]{:S(2)}) copy-start(s32[512]{0:T(512)} %param.13) | copy-start | bytes 6148
  66.6 18.3 %all-to-all-start = ((bf16[128,3,8,128]{3,0,1,2:T(8,128)(2,1)}), bf16[128,3,8,128]{3,0,1,2:T(8,128)(2,1)S(1)}, u32[]{:S(2)}, u32[]{:S(2)}) async-start(bf16[128,3,8,128]{3,0,1,2:T(8,128)(2,1)} %copy.76), calls=%async_computation | async-start | bytes 1572864 | tf_op jit(solution)/shard_map/all_to_all | solution.py:46
  72.3 50.2 %all-gather.9.cloned.1.call-start = ((), (), s32[]{:S(2)}) async-start(), calls=%async_computation.5 | async-start | bytes 1114112 | tf_op jit(solution)/shard_map/all_gather | solution.py:43
  73.1 383.4 %all-gather.11.cloned.1.call-start = ((), (), s32[]{:S(2)}) async-start(), calls=%async_computation.6 | async-start | bytes 18874368 | tf_op jit(solution)/shard_map/all_gather | solution.py:8
  85.6 1.2 copy-start
  87.6 4.9 copy-start.2
  87.6 4.9 copy-start.3
  87.6 4.9 collective-permute-start
  89.1 3.4 collective-permute-start.1
  89.8 0.8 copy-start.10
  96.5 26.0 %all-to-all-start.2 = ((bf16[128,1,8,512]{3,0,1,2:T(8,128)(2,1)}), bf16[128,1,8,512]{3,0,1,2:T(8,128)(2,1)S(1)}, u32[]{:S(2)}, u32[]{:S(2)}) async-start(bf16[128,1,8,512]{3,0,1,2:T(8,128)(2,1)} %all-gather.7.cloned.1.call-done), calls=%async_computation.2 | async-start | bytes 2097152 | tf_op jit(solution)/shard_map/all_to_all | solution.py:48
  122.6 25.4 %all-to-all-start.3 = ((bf16[128,1,8,512]{3,0,1,2:T(8,128)(2,1)}), bf16[128,1,8,512]{3,0,1,2:T(8,128)(2,1)S(1)}, u32[]{:S(2)}, u32[]{:S(2)}) async-start(bf16[128,1,8,512]{3,0,1,2:T(8,128)(2,1)} %all-gather.9.cloned.1.call-done), calls=%async_computation.3 | async-start | bytes 2097152 | tf_op jit(solution)/shard_map/all_to_all | solution.py:49
  127.2 672.2 %all-gather.13.cloned.1.call-start = ((), (), s32[]{:S(2)}) async-start(), calls=%async_computation.7 | async-start | bytes 18874368 | tf_op jit(solution)/shard_map/all_gather | solution.py:8
  464.7 0.7 copy-start.6
  464.7 0.7 copy-start.7
  799.4 8.0 copy-start.1
  807.8 0.7 copy-start.8
  807.8 0.7 copy-start.9
Sparse Core Ops, SparseCore 0:
  10.3 50.6 all-gather.6
  76.0 46.5 all-gather.8
  124.2 332.2 all-gather.10
  473.6 325.7 all-gather.12
